TPU v7x, 512 devices: a whole 4x8x8 slice. The times are simulated.
512 devices in a mesh: row: 64 (over z, y), col: 8 (over x, core).
Axes of the slice: x: 4, y: 8, z: 8, core: 2. Of those that a mesh axis runs over, the one named last changes fastest.
Arguments:
- dinv0: bfloat16 [65536, 4096], P('row', 'col'), as said below
- dinv1: bfloat16 [32768, 4096], P('row', 'col'), as said below
- dinv2: bfloat16 [16384, 4096], P('row', 'col'), as said below
- offdiag0: bfloat16 [65536, 4096], P('row', 'col'), may hold values from -0.0625 to 0.0625
- offdiag1: bfloat16 [32768, 4096], P('row', 'col'), may hold values from -0.0625 to 0.0625
- rhs0: bfloat16 [65536, 128], P(('row', 'col')), may hold values from -6 to 6
- rhs1: bfloat16 [32768, 128], P(('row', 'col')), may hold values from -6 to 6
- rhs2: bfloat16 [16384, 128], P(('row', 'col')), may hold values from -6 to 6
- block_rows0: int32 [16, 64, 16], replicated, may hold values from 0 to 63, all different within a row
- block_rows1: int32 [8, 64, 16], replicated, may hold values from 0 to 63, all different within a row
Outputs:
- solution0: float32 [65536, 128], P(('row', 'col'))
- solution1: float32 [32768, 128], P(('row', 'col'))
- solution2: float32 [16384, 128], P(('row', 'col'))
Inputs may be any that keep to these rules, and one draw needn't show every extreme that they name: `block_rows0`: each row of the last dimension lists 16 different block rows. `block_rows1`: each row of the last dimension lists 16 different block rows. `dinv0`: each supernode's block is lower triangular in global order, with a positive diagonal. `dinv1`: each supernode's block is lower triangular in global order, with a positive diagonal. `dinv2`: each supernode's block is lower triangular in global order, with a positive diagonal.
All inputs are finite; a program needn't handle non-finite values.
Results may differ from a plain program's by a relative error of at most 0.0095.
Values may be sent and summed in bfloat16 or wider, within the bound.
No kernel may reach another device: no remote copies, remote signals or barrier semaphores. Data moves between devices by JAX's collectives and lax.ppermute only.
A program may use at most 64 MiB of HBM per device.

v0:
```python
import jax
import jax.numpy as jnp
from jax import lax
from jax.sharding import PartitionSpec as P

MB = 64
GR = 4


def partner(value, axis, stride):
    return lax.ppermute(value, axis, [(i, i ^ 1 << stride) for i in range(lax.axis_size(axis))])


def own_bit(which):
    return lax.axis_index("row") >> which & 1


def row_join(pieces, depth):
    joined = pieces
    for which in range(depth):
        other = partner(joined, "row", which)
        first = jnp.concatenate((joined, other), axis=1)
        second = jnp.concatenate((other, joined), axis=1)
        joined = jnp.where(own_bit(which) == 0, first, second)
    return joined.reshape(-1, joined.shape[-1])


def row_fold(partial_value, row_blocks, depth):
    width = partial_value.shape[-1]
    folded = partial_value.reshape(row_blocks, 1 << depth, -1, width)
    for which in range(depth):
        halves = folded.reshape(row_blocks, folded.shape[1] // 2, 2, folded.shape[2], width)
        mine = own_bit(which)
        keeping = lax.dynamic_index_in_dim(halves, mine, 2, keepdims=False)
        sending = lax.dynamic_index_in_dim(halves, 1 - mine, 2, keepdims=False)
        folded = keeping + partner(sending.astype(jnp.bfloat16), "row", which).astype(sending.dtype)
    return folded


def column_sum(partial_value, col_devs):
    width = partial_value.shape[-1]
    shaped = partial_value.reshape(-1, col_devs, MB // col_devs, width)
    return lax.psum_scatter(shaped, "col", scatter_dimension=1, tiled=True)


def column_join(pieces):
    gathered = lax.all_gather(pieces, "col", axis=1, tiled=True)
    return gathered.reshape(-1, gathered.shape[-1])


def sibling_fold(values, which):
    mine = own_bit(which)
    keeping = lax.dynamic_index_in_dim(values, mine, 1, keepdims=True)
    sending = lax.dynamic_index_in_dim(values, 1 - mine, 1, keepdims=True)
    return keeping + partner(sending.astype(jnp.bfloat16), "row", which).astype(sending.dtype)


def parent_rows(values, which):
    other = partner(values, "row", which)
    first = jnp.concatenate((values, other), axis=1)
    second = jnp.concatenate((other, values), axis=1)
    joined = jnp.where(own_bit(which) == 0, first, second)
    return joined.reshape(joined.shape[0] * 2, 1, joined.shape[2], joined.shape[3])


def coupling(values, listings, depth):
    row_count = values.shape[0]
    row_blocks = row_count // MB
    group = 1 << depth
    position = lax.axis_index("row")
    member = position // group
    local = position % group
    owned = jnp.arange(row_blocks, dtype=jnp.int32) * group + local
    listing = lax.dynamic_index_in_dim(listings, member, 0, keepdims=False)
    listed = jnp.any(listing[None, :, :] == owned[:, None, None], axis=-1)
    unit_width = values.shape[1] // listed.shape[1]
    keeping = jnp.repeat(jnp.repeat(listed, MB, axis=0), unit_width, axis=1)
    return jnp.where(keeping, values, jnp.zeros_like(values))


def per_device(dinv0, dinv1, dinv2, offdiag0, offdiag1, rhs0, rhs1, rhs2, block_rows0, block_rows1):
    col_devs = lax.axis_size("col")
    col_width = MB // col_devs
    width = rhs0.shape[1]
    lowest = GR.bit_length() - 1
    depths = (lowest, lowest + 1, lowest + 2)
    inverses = (dinv0, dinv1, dinv2)
    couplings = (
        coupling(offdiag0, block_rows0, depths[0]),
        coupling(offdiag1, block_rows1, depths[1]),
    )
    sides = (rhs0, rhs1, rhs2)

    def as_pieces(values):
        return values.reshape(-1, 1, col_width, width)

    solved = []
    residual = as_pieces(rhs0)
    for level in range(3):
        column_form = row_join(residual, depths[level])
        product = jnp.dot(inverses[level], column_form, preferred_element_type=jnp.float32)
        solved_pieces = column_sum(product, col_devs).astype(jnp.bfloat16)
        solved.append(solved_pieces)
        if level < 2:
            solved_columns = row_join(solved_pieces, depths[level])
            partial_value = jnp.dot(
                couplings[level], solved_columns, preferred_element_type=jnp.float32
            )
            summed = column_sum(partial_value, col_devs)
            summed = summed.reshape(summed.shape[0] // 2, 2, col_width, width)
            update = sibling_fold(summed, depths[level])
            residual = (as_pieces(sides[level + 1]).astype(jnp.float32) - update).astype(
                jnp.bfloat16
            )
    outputs = [None, None, None]
    weighted = solved[2]
    for level in (2, 1, 0):
        row_form = column_join(weighted)
        product = jnp.einsum(
            "ij,in->jn", inverses[level], row_form, preferred_element_type=jnp.float32
        )
        answer = row_fold(product, row_form.shape[0] // MB, depths[level])
        outputs[level] = answer.reshape(-1, width)
        if level > 0:
            child_pieces = parent_rows(answer.astype(jnp.bfloat16), depths[level - 1])
            child_form = column_join(child_pieces)
            partial_value = jnp.einsum(
                "ij,in->jn", couplings[level - 1], child_form, preferred_element_type=jnp.float32
            )
            carried = row_fold(partial_value, child_form.shape[0] // MB, depths[level - 1])
            weighted = (solved[level - 1].astype(jnp.float32) - carried).astype(jnp.bfloat16)
    return (outputs[0], outputs[1], outputs[2])


def solution(mesh):
    placed = (
        P("row", "col"),
        P("row", "col"),
        P("row", "col"),
        P("row", "col"),
        P("row", "col"),
        P(("row", "col"), None),
        P(("row", "col"), None),
        P(("row", "col"), None),
        P(),
        P(),
    )
    return jax.shard_map(
        per_device,
        mesh=mesh,
        in_specs=placed,
        out_specs=(P(("row", "col"), None), P(("row", "col"), None), P(("row", "col"), None)),
        check_vma=False,
    )
```

profile of v0, /device:TPU:24, one launch (start us, length us, event | category | flops | bytes accessed | tf_op | source)
XLA Modules:
  0.0 549.9 jit_solution(3072285865795595267)
XLA Ops:
  13.4 6.0 %collective-permute-start.1 = (bf16[16,2,8,128]{3,2,1,0:T(8,128)(2,1)S(1)}, bf16[16,2,8,128]{3,2,1,0:T(8,128)(2,1)S(1)}, u32[]{:S(2)}, u32[]{:S(2)}) collective-permute-start(bf16[16,2,8,128]{3,2,1,0:T(8,128)(2,1)S(1)} %maximum_select_fusion.5), channel_id=1, source_target_pairs={{0,16},{8,24},{16,0},{24,8},{32,48},{40,56},{48,32},{56,40},{64,80... | collective-permute-start | bytes 196616 | tf_op jit(solution)/shard_map/ppermute | solution.py:11
  22.4 29.2 %all-reduce.14 = bf16[16,8,8,128]{3,2,1,0:T(8,128)(2,1)S(1)} all-reduce(f32[16,8,8,128]{3,2,1,0:T(8,128)S(1)} %bitcast.169), channel_id=2, replica_groups=mesh['row'=64,'col'=8] {'col'}, use_global_device_ids=true, to_apply=%region_0.1.clone | all-reduce | flops 131072 | bytes 786432
  52.2 4.1 collective-permute-start.2
  58.5 4.8 collective-permute-start.3
  66.9 73.2 %all-reduce.11.cloned.1.call-done = f32[16,8,8,128]{3,2,1,0:T(8,128)} async-done(((f32[16,8,8,128]{3,2,1,0:T(8,128)}), f32[16,8,8,128]{3,2,1,0:T(8,128)}) %all-reduce.11.cloned.1.call-update) | async-done | bytes 524304
  141.6 4.7 collective-permute-start.4
  146.2 4.9 collective-permute-done.4
  159.2 4.3 collective-permute-done.6
  163.5 4.8 collective-permute-start.7
  169.0 4.6 collective-permute-done.7
  174.0 26.3 %all-reduce.15 = bf16[8,8,8,128]{3,2,1,0:T(8,128)(2,1)S(1)} all-reduce(f32[8,8,8,128]{3,2,1,0:T(8,128)S(1)} %bitcast.170), channel_id=4, replica_groups=mesh['row'=64,'col'=8] {'col'}, use_global_device_ids=true, to_apply=%region_3.4.clone | all-reduce | flops 65536 | bytes 393216
  213.3 5.6 %collective-permute-start.10 = (bf16[8,4,8,128]{3,2,1,0:T(8,128)(2,1)S(1)}, bf16[8,4,8,128]{3,2,1,0:T(8,128)(2,1)S(1)}, u32[]{:S(2)}, u32[]{:S(2)}) collective-permute-start(bf16[8,4,8,128]{3,2,1,0:T(8,128)(2,1)S(1)} %maximum_select_fusion.8), channel_id=1, source_target_pairs={{0,32},{8,40},{16,48},{24,56},{32,0},{40,8},{48,16},{56,24},{64,96... | collective-permute-start | bytes 196616 | tf_op jit(solution)/shard_map/ppermute | solution.py:11
  225.5 72.1 %all-reduce.13.cloned.1.call-done = f32[8,8,8,128]{3,2,1,0:T(8,128)} async-done(((f32[8,8,8,128]{3,2,1,0:T(8,128)}), f32[8,8,8,128]{3,2,1,0:T(8,128)}) %all-reduce.13.cloned.1.call-update) | async-done | bytes 262160
  312.8 4.3 collective-permute-done.13
  317.1 4.5 collective-permute-start.14
  321.6 5.2 collective-permute-done.14
  334.9 25.3 %all-reduce.16 = bf16[4,8,8,128]{3,2,1,0:T(8,128)(2,1)} all-reduce(f32[4,8,8,128]{3,2,1,0:T(8,128)S(1)} %bitcast.183), channel_id=6, replica_groups=mesh['row'=64,'col'=8] {'col'}, use_global_device_ids=true, to_apply=%region_6.7.clone | all-reduce | flops 32768 | bytes 196608
  361.5 11.2 %all_gather.15 = bf16[4,8,8,128]{3,2,1,0:T(8,128)(2,1)S(1)} all-gather(bf16[4,1,8,128]{3,2,1,0:T(8,128)(2,1)S(1)} %dynamic-slice_convert_fusion.14), channel_id=1, replica_groups=mesh['row'=64,'col'=8] {'col'}, dimensions={1}, use_global_device_ids=true | all-gather | bytes 73728 | tf_op jit(solution)/shard_map/all_gather | solution.py:47
  384.2 4.8 collective-permute-done.17
  389.0 4.2 collective-permute-start.18
  393.2 5.4 collective-permute-done.18
  410.3 11.3 %all_gather.16 = bf16[8,8,8,128]{3,2,1,0:T(8,128)(2,1)S(1)} all-gather(bf16[8,1,8,128]{3,2,1,0:T(8,128)(2,1)S(1)} %bitcast.201), channel_id=1, replica_groups=mesh['row'=64,'col'=8] {'col'}, dimensions={1}, use_global_device_ids=true | all-gather | bytes 147456 | tf_op jit(solution)/shard_map/all_gather | solution.py:47
  430.1 5.1 collective-permute-done.22
  439.1 5.7 %collective-permute-done.23 = bf16[8,1,8,128]{3,2,1,0:T(8,128)(2,1)S(1)} collective-permute-done((bf16[8,1,8,128]{3,2,1,0:T(8,128)(2,1)S(1)}, bf16[8,1,8,128]{3,2,1,0:T(8,128)(2,1)S(1)}, u32[]{:S(2)}, u32[]{:S(2)}) %collective-permute-start.23) | collective-permute-done | bytes 16416 | tf_op jit(solution)/shard_map/ppermute | solution.py:11
  446.2 11.3 %all_gather.17 = bf16[8,8,8,128]{3,2,1,0:T(8,128)(2,1)S(1)} all-gather(bf16[8,1,8,128]{3,2,1,0:T(8,128)(2,1)S(1)} %subtract_convert_fusion.1), channel_id=1, replica_groups=mesh['row'=64,'col'=8] {'col'}, dimensions={1}, use_global_device_ids=true | all-gather | bytes 147456 | tf_op jit(solution)/shard_map/all_gather | solution.py:47
  466.1 4.9 collective-permute-done.25
  474.8 5.8 %collective-permute-done.26 = bf16[8,1,8,128]{3,2,1,0:T(8,128)(2,1)S(1)} collective-permute-done((bf16[8,1,8,128]{3,2,1,0:T(8,128)(2,1)S(1)}, bf16[8,1,8,128]{3,2,1,0:T(8,128)(2,1)S(1)}, u32[]{:S(2)}, u32[]{:S(2)}) %collective-permute-start.26) | collective-permute-done | bytes 16416 | tf_op jit(solution)/shard_map/ppermute | solution.py:11
  484.9 5.8 %collective-permute-done.27 = bf16[8,1,8,128]{3,2,1,0:T(8,128)(2,1)S(1)} collective-permute-done((bf16[8,1,8,128]{3,2,1,0:T(8,128)(2,1)S(1)}, bf16[8,1,8,128]{3,2,1,0:T(8,128)(2,1)S(1)}, u32[]{:S(2)}, u32[]{:S(2)}) %collective-permute-start.27) | collective-permute-done | bytes 16416 | tf_op jit(solution)/shard_map/ppermute | solution.py:11
  490.7 11.6 %all_gather.18 = bf16[16,8,8,128]{3,2,1,0:T(8,128)(2,1)S(1)} all-gather(bf16[16,1,8,128]{3,2,1,0:T(8,128)(2,1)S(1)} %bitcast.198), channel_id=1, replica_groups=mesh['row'=64,'col'=8] {'col'}, dimensions={1}, use_global_device_ids=true | all-gather | bytes 294912 | tf_op jit(solution)/shard_map/all_gather | solution.py:47
  511.0 4.9 collective-permute-done.29
  517.2 11.6 %all_gather.19 = bf16[16,8,8,128]{3,2,1,0:T(8,128)(2,1)S(1)} all-gather(bf16[16,1,8,128]{3,2,1,0:T(8,128)(2,1)S(1)} %subtract_convert_fusion), channel_id=1, replica_groups=mesh['row'=64,'col'=8] {'col'}, dimensions={1}, use_global_device_ids=true | all-gather | bytes 294912 | tf_op jit(solution)/shard_map/all_gather | solution.py:47
  537.5 4.9 collective-permute-done.31
  (150 shorter events, 143.2 us)
Async XLA Ops:
  7.2 132.9 %all-reduce.11.cloned.1.call-start = ((), (), s32[]{:S(2)}) async-start(), calls=%async_computation | async-start | bytes 1048576
  7.2 6.2 %collective-permute-start = (bf16[16,1,8,128]{3,2,1,0:T(8,128)(2,1)}, bf16[16,1,8,128]{3,2,1,0:T(8,128)(2,1)S(1)}, u32[]{:S(2)}, u32[]{:S(2)}) collective-permute-start(bf16[16,1,8,128]{3,2,1,0:T(8,128)(2,1)} %bitcast.202), channel_id=1, source_target_pairs={{0,8},{8,0},{16,24},{24,16},{32,40},{40,32},{48,56},{56,48},{64,72... | collective-permute-start | bytes 98312 | tf_op jit(solution)/shard_map/ppermute | solution.py:11
  13.4 8.3 %collective-permute-start.1 = (bf16[16,2,8,128]{3,2,1,0:T(8,128)(2,1)S(1)}, bf16[16,2,8,128]{3,2,1,0:T(8,128)(2,1)S(1)}, u32[]{:S(2)}, u32[]{:S(2)}) collective-permute-start(bf16[16,2,8,128]{3,2,1,0:T(8,128)(2,1)S(1)} %maximum_select_fusion.5), channel_id=1, source_target_pairs={{0,16},{8,24},{16,0},{24,8},{32,48},{40,56},{48,32},{56,40},{64,80... | collective-permute-start | bytes 196616 | tf_op jit(solution)/shard_map/ppermute | solution.py:11
  52.2 6.3 %collective-permute-start.2 = (bf16[16,1,8,128]{3,2,1,0:T(8,128)(2,1)S(1)}, bf16[16,1,8,128]{3,2,1,0:T(8,128)(2,1)S(1)}, u32[]{:S(2)}, u32[]{:S(2)}) collective-permute-start(bf16[16,1,8,128]{3,2,1,0:T(8,128)(2,1)S(1)} %dynamic-slice_convert_fusion.5), channel_id=1, source_target_pairs={{0,8},{8,0},{16,24},{24,16},{32,40},{40,32},{48,56},{56,48},{64,72... | collective-permute-start | bytes 98312 | tf_op jit(solution)/shard_map/ppermute | solution.py:11
  58.5 7.1 %collective-permute-start.3 = (bf16[16,2,8,128]{3,2,1,0:T(8,128)(2,1)S(1)}, bf16[16,2,8,128]{3,2,1,0:T(8,128)(2,1)S(1)}, u32[]{:S(2)}, u32[]{:S(2)}) collective-permute-start(bf16[16,2,8,128]{3,2,1,0:T(8,128)(2,1)S(1)} %maximum_select_fusion.6), channel_id=1, source_target_pairs={{0,16},{8,24},{16,0},{24,8},{32,48},{40,56},{48,32},{56,40},{64,80... | collective-permute-start | bytes 196616 | tf_op jit(solution)/shard_map/ppermute | solution.py:11
  66.9 230.8 %all-reduce.13.cloned.1.call-start = ((), (), s32[]{:S(2)}) async-start(), calls=%async_computation.1 | async-start | bytes 524288
  141.6 9.5 %collective-permute-start.4 = (bf16[8,1,8,128]{3,2,1,0:T(8,128)(2,1)S(1)}, bf16[8,1,8,128]{3,2,1,0:T(8,128)(2,1)S(1)}, u32[]{:S(2)}, u32[]{:S(2)}) collective-permute-start(bf16[8,1,8,128]{3,2,1,0:T(8,128)(2,1)S(1)} %dynamic-slice_convert_fusion.13), channel_id=1, source_target_pairs={{0,32},{8,40},{16,48},{24,56},{32,0},{40,8},{48,16},{56,24},{64,96... | collective-permute-start | bytes 49160 | tf_op jit(solution)/shard_map/ppermute | solution.py:11
  151.1 5.6 %collective-permute-start.5 = (bf16[8,1,8,128]{3,2,1,0:T(8,128)(2,1)S(1)}, bf16[8,1,8,128]{3,2,1,0:T(8,128)(2,1)S(1)}, u32[]{:S(2)}, u32[]{:S(2)}) collective-permute-start(bf16[8,1,8,128]{3,2,1,0:T(8,128)(2,1)S(1)} %fusion.8), channel_id=1, source_target_pairs={{0,8},{8,0},{16,24},{24,16},{32,40},{40,32},{48,56},{56,48},{64,72... | collective-permute-start | bytes 49160 | tf_op jit(solution)/shard_map/ppermute | solution.py:11
  156.8 6.7 %collective-permute-start.6 = (bf16[8,2,8,128]{3,2,1,0:T(8,128)(2,1)S(1)}, bf16[8,2,8,128]{3,2,1,0:T(8,128)(2,1)S(1)}, u32[]{:S(2)}, u32[]{:S(2)}) collective-permute-start(bf16[8,2,8,128]{3,2,1,0:T(8,128)(2,1)S(1)} %maximum_select_fusion.10), channel_id=1, source_target_pairs={{0,16},{8,24},{16,0},{24,8},{32,48},{40,56},{48,32},{56,40},{64,80... | collective-permute-start | bytes 98312 | tf_op jit(solution)/shard_map/ppermute | solution.py:11
  163.5 10.1 %collective-permute-start.7 = (bf16[8,4,8,128]{3,2,1,0:T(8,128)(2,1)S(1)}, bf16[8,4,8,128]{3,2,1,0:T(8,128)(2,1)S(1)}, u32[]{:S(2)}, u32[]{:S(2)}) collective-permute-start(bf16[8,4,8,128]{3,2,1,0:T(8,128)(2,1)S(1)} %maximum_select_fusion.7), channel_id=1, source_target_pairs={{0,32},{8,40},{16,48},{24,56},{32,0},{40,8},{48,16},{56,24},{64,96... | collective-permute-start | bytes 196616 | tf_op jit(solution)/shard_map/ppermute | solution.py:11
  201.0 5.6 %collective-permute-start.8 = (bf16[8,1,8,128]{3,2,1,0:T(8,128)(2,1)S(1)}, bf16[8,1,8,128]{3,2,1,0:T(8,128)(2,1)S(1)}, u32[]{:S(2)}, u32[]{:S(2)}) collective-permute-start(bf16[8,1,8,128]{3,2,1,0:T(8,128)(2,1)S(1)} %dynamic-slice_convert_fusion.9), channel_id=1, source_target_pairs={{0,8},{8,0},{16,24},{24,16},{32,40},{40,32},{48,56},{56,48},{64,72... | collective-permute-start | bytes 49160 | tf_op jit(solution)/shard_map/ppermute | solution.py:11
  206.6 6.7 %collective-permute-start.9 = (bf16[8,2,8,128]{3,2,1,0:T(8,128)(2,1)S(1)}, bf16[8,2,8,128]{3,2,1,0:T(8,128)(2,1)S(1)}, u32[]{:S(2)}, u32[]{:S(2)}) collective-permute-start(bf16[8,2,8,128]{3,2,1,0:T(8,128)(2,1)S(1)} %maximum_select_fusion.11), channel_id=1, source_target_pairs={{0,16},{8,24},{16,0},{24,8},{32,48},{40,56},{48,32},{56,40},{64,80... | collective-permute-start | bytes 98312 | tf_op jit(solution)/shard_map/ppermute | solution.py:11
  213.3 10.1 %collective-permute-start.10 = (bf16[8,4,8,128]{3,2,1,0:T(8,128)(2,1)S(1)}, bf16[8,4,8,128]{3,2,1,0:T(8,128)(2,1)S(1)}, u32[]{:S(2)}, u32[]{:S(2)}) collective-permute-start(bf16[8,4,8,128]{3,2,1,0:T(8,128)(2,1)S(1)} %maximum_select_fusion.8), channel_id=1, source_target_pairs={{0,32},{8,40},{16,48},{24,56},{32,0},{40,8},{48,16},{56,24},{64,96... | collective-permute-start | bytes 196616 | tf_op jit(solution)/shard_map/ppermute | solution.py:11
  299.0 5.7 %collective-permute-start.11 = (bf16[4,1,8,128]{3,2,1,0:T(8,128)(2,1)S(1)}, bf16[4,1,8,128]{3,2,1,0:T(8,128)(2,1)S(1)}, u32[]{:S(2)}, u32[]{:S(2)}) collective-permute-start(bf16[4,1,8,128]{3,2,1,0:T(8,128)(2,1)S(1)} %dynamic-slice_convert_fusion.16), channel_id=1, source_target_pairs={{0,64},{8,72},{16,80},{24,88},{32,96},{40,104},{48,112},{56,120},{... | collective-permute-start | bytes 24584 | tf_op jit(solution)/shard_map/ppermute | solution.py:11
  304.7 5.7 %collective-permute-start.12 = (bf16[4,1,8,128]{3,2,1,0:T(8,128)(2,1)S(1)}, bf16[4,1,8,128]{3,2,1,0:T(8,128)(2,1)S(1)}, u32[]{:S(2)}, u32[]{:S(2)}) collective-permute-start(bf16[4,1,8,128]{3,2,1,0:T(8,128)(2,1)S(1)} %fusion.12), channel_id=1, source_target_pairs={{0,8},{8,0},{16,24},{24,16},{32,40},{40,32},{48,56},{56,48},{64,72... | collective-permute-start | bytes 24584 | tf_op jit(solution)/shard_map/ppermute | solution.py:11
  310.4 6.7 %collective-permute-start.13 = (bf16[4,2,8,128]{3,2,1,0:T(8,128)(2,1)S(1)}, bf16[4,2,8,128]{3,2,1,0:T(8,128)(2,1)S(1)}, u32[]{:S(2)}, u32[]{:S(2)}) collective-permute-start(bf16[4,2,8,128]{3,2,1,0:T(8,128)(2,1)S(1)} %maximum_select_fusion.14), channel_id=1, source_target_pairs={{0,16},{8,24},{16,0},{24,8},{32,48},{40,56},{48,32},{56,40},{64,80... | collective-permute-start | bytes 49160 | tf_op jit(solution)/shard_map/ppermute | solution.py:11
  317.1 9.7 %collective-permute-start.14 = (bf16[4,4,8,128]{3,2,1,0:T(8,128)(2,1)S(1)}, bf16[4,4,8,128]{3,2,1,0:T(8,128)(2,1)S(1)}, u32[]{:S(2)}, u32[]{:S(2)}) collective-permute-start(bf16[4,4,8,128]{3,2,1,0:T(8,128)(2,1)S(1)} %maximum_select_fusion.12), channel_id=1, source_target_pairs={{0,32},{8,40},{16,48},{24,56},{32,0},{40,8},{48,16},{56,24},{64,96... | collective-permute-start | bytes 98312 | tf_op jit(solution)/shard_map/ppermute | solution.py:11
  326.8 6.2 %collective-permute-start.15 = (bf16[4,8,8,128]{3,2,1,0:T(8,128)(2,1)S(1)}, bf16[4,8,8,128]{3,2,1,0:T(8,128)(2,1)S(1)}, u32[]{:S(2)}, u32[]{:S(2)}) collective-permute-start(bf16[4,8,8,128]{3,2,1,0:T(8,128)(2,1)S(1)} %maximum_select_fusion.9), channel_id=1, source_target_pairs={{0,64},{8,72},{16,80},{24,88},{32,96},{40,104},{48,112},{56,120},{... | collective-permute-start | bytes 196616 | tf_op jit(solution)/shard_map/ppermute | solution.py:11
  374.7 6.3 %collective-permute-start.16 = (bf16[4,8,8,128]{3,2,1,0:T(8,128)(2,1)S(1)}, bf16[4,8,8,128]{3,2,1,0:T(8,128)(2,1)}, u32[]{:S(2)}, u32[]{:S(2)}) collective-permute-start(bf16[4,8,8,128]{3,2,1,0:T(8,128)(2,1)S(1)} %fusion), channel_id=1, source_target_pairs={{0,8},{8,0},{16,24},{24,16},{32,40},{40,32},{48,56},{56,48},{64,72... | collective-permute-start | bytes 196616 | tf_op jit(solution)/shard_map/ppermute | solution.py:11
  381.9 7.1 %collective-permute-start.17 = (bf16[4,4,8,128]{3,2,1,0:T(8,128)(2,1)S(1)}, bf16[4,4,8,128]{3,2,1,0:T(8,128)(2,1)S(1)}, u32[]{:S(2)}, u32[]{:S(2)}) collective-permute-start(bf16[4,4,8,128]{3,2,1,0:T(8,128)(2,1)S(1)} %fusion.6), channel_id=1, source_target_pairs={{0,16},{8,24},{16,0},{24,8},{32,48},{40,56},{48,32},{56,40},{64,80... | collective-permute-start | bytes 98312 | tf_op jit(solution)/shard_map/ppermute | solution.py:11
  389.0 9.5 %collective-permute-start.18 = (bf16[4,2,8,128]{3,2,1,0:T(8,128)(2,1)S(1)}, bf16[4,2,8,128]{3,2,1,0:T(8,128)(2,1)S(1)}, u32[]{:S(2)}, u32[]{:S(2)}) collective-permute-start(bf16[4,2,8,128]{3,2,1,0:T(8,128)(2,1)S(1)} %fusion.11), channel_id=1, source_target_pairs={{0,32},{8,40},{16,48},{24,56},{32,0},{40,8},{48,16},{56,24},{64,96... | collective-permute-start | bytes 49160 | tf_op jit(solution)/shard_map/ppermute | solution.py:11
  421.9 6.2 %collective-permute-start.21 = (bf16[8,4,8,128]{3,2,1,0:T(8,128)(2,1)S(1)}, bf16[8,4,8,128]{3,2,1,0:T(8,128)(2,1)S(1)}, u32[]{:S(2)}, u32[]{:S(2)}) collective-permute-start(bf16[8,4,8,128]{3,2,1,0:T(8,128)(2,1)S(1)} %fusion.1), channel_id=1, source_target_pairs={{0,8},{8,0},{16,24},{24,16},{32,40},{40,32},{48,56},{56,48},{64,72... | collective-permute-start | bytes 196616 | tf_op jit(solution)/shard_map/ppermute | solution.py:11
  428.2 7.0 %collective-permute-start.22 = (bf16[8,2,8,128]{3,2,1,0:T(8,128)(2,1)S(1)}, bf16[8,2,8,128]{3,2,1,0:T(8,128)(2,1)S(1)}, u32[]{:S(2)}, u32[]{:S(2)}) collective-permute-start(bf16[8,2,8,128]{3,2,1,0:T(8,128)(2,1)S(1)} %fusion.7), channel_id=1, source_target_pairs={{0,16},{8,24},{16,0},{24,8},{32,48},{40,56},{48,32},{56,40},{64,80... | collective-permute-start | bytes 98312 | tf_op jit(solution)/shard_map/ppermute | solution.py:11
  435.3 9.5 %collective-permute-start.23 = (bf16[8,1,8,128]{3,2,1,0:T(8,128)(2,1)S(1)}, bf16[8,1,8,128]{3,2,1,0:T(8,128)(2,1)S(1)}, u32[]{:S(2)}, u32[]{:S(2)}) collective-permute-start(bf16[8,1,8,128]{3,2,1,0:T(8,128)(2,1)S(1)} %dynamic-slice_convert_fusion.11), channel_id=1, source_target_pairs={{0,32},{8,40},{16,48},{24,56},{32,0},{40,8},{48,16},{56,24},{64,96... | collective-permute-start | bytes 49160 | tf_op jit(solution)/shard_map/ppermute | solution.py:11
  457.9 6.2 %collective-permute-start.24 = (bf16[8,4,8,128]{3,2,1,0:T(8,128)(2,1)S(1)}, bf16[8,4,8,128]{3,2,1,0:T(8,128)(2,1)S(1)}, u32[]{:S(2)}, u32[]{:S(2)}) collective-permute-start(bf16[8,4,8,128]{3,2,1,0:T(8,128)(2,1)S(1)} %fusion.2), channel_id=1, source_target_pairs={{0,8},{8,0},{16,24},{24,16},{32,40},{40,32},{48,56},{56,48},{64,72... | collective-permute-start | bytes 196616 | tf_op jit(solution)/shard_map/ppermute | solution.py:11
  464.2 6.8 %collective-permute-start.25 = (bf16[8,2,8,128]{3,2,1,0:T(8,128)(2,1)S(1)}, bf16[8,2,8,128]{3,2,1,0:T(8,128)(2,1)S(1)}, u32[]{:S(2)}, u32[]{:S(2)}) collective-permute-start(bf16[8,2,8,128]{3,2,1,0:T(8,128)(2,1)S(1)} %fusion.5), channel_id=1, source_target_pairs={{0,16},{8,24},{16,0},{24,8},{32,48},{40,56},{48,32},{56,40},{64,80... | collective-permute-start | bytes 98312 | tf_op jit(solution)/shard_map/ppermute | solution.py:11
  471.0 9.5 %collective-permute-start.26 = (bf16[8,1,8,128]{3,2,1,0:T(8,128)(2,1)S(1)}, bf16[8,1,8,128]{3,2,1,0:T(8,128)(2,1)S(1)}, u32[]{:S(2)}, u32[]{:S(2)}) collective-permute-start(bf16[8,1,8,128]{3,2,1,0:T(8,128)(2,1)S(1)} %dynamic-slice_convert_fusion.10), channel_id=1, source_target_pairs={{0,32},{8,40},{16,48},{24,56},{32,0},{40,8},{48,16},{56,24},{64,96... | collective-permute-start | bytes 49160 | tf_op jit(solution)/shard_map/ppermute | solution.py:11
  481.1 9.5 %collective-permute-start.27 = (bf16[8,1,8,128]{3,2,1,0:T(8,128)(2,1)S(1)}, bf16[8,1,8,128]{3,2,1,0:T(8,128)(2,1)S(1)}, u32[]{:S(2)}, u32[]{:S(2)}) collective-permute-start(bf16[8,1,8,128]{3,2,1,0:T(8,128)(2,1)S(1)} %get-tuple-element.4), channel_id=1, source_target_pairs={{0,32},{8,40},{16,48},{24,56},{32,0},{40,8},{48,16},{56,24},{64,96... | collective-permute-start | bytes 49160 | tf_op jit(solution)/shard_map/ppermute | solution.py:11
  502.8 6.2 %collective-permute-start.28 = (bf16[16,2,8,128]{3,2,1,0:T(8,128)(2,1)S(1)}, bf16[16,2,8,128]{3,2,1,0:T(8,128)(2,1)S(1)}, u32[]{:S(2)}, u32[]{:S(2)}) collective-permute-start(bf16[16,2,8,128]{3,2,1,0:T(8,128)(2,1)S(1)} %fusion.3), channel_id=1, source_target_pairs={{0,8},{8,0},{16,24},{24,16},{32,40},{40,32},{48,56},{56,48},{64,72... | collective-permute-start | bytes 196616 | tf_op jit(solution)/shard_map/ppermute | solution.py:11
  509.0 6.8 %collective-permute-start.29 = (bf16[16,1,8,128]{3,2,1,0:T(8,128)(2,1)S(1)}, bf16[16,1,8,128]{3,2,1,0:T(8,128)(2,1)S(1)}, u32[]{:S(2)}, u32[]{:S(2)}) collective-permute-start(bf16[16,1,8,128]{3,2,1,0:T(8,128)(2,1)S(1)} %dynamic-slice_convert_fusion.7), channel_id=1, source_target_pairs={{0,16},{8,24},{16,0},{24,8},{32,48},{40,56},{48,32},{56,40},{64,80... | collective-permute-start | bytes 98312 | tf_op jit(solution)/shard_map/ppermute | solution.py:11
  529.3 6.2 %collective-permute-start.30 = (bf16[16,2,8,128]{3,2,1,0:T(8,128)(2,1)S(1)}, bf16[16,2,8,128]{3,2,1,0:T(8,128)(2,1)S(1)}, u32[]{:S(2)}, u32[]{:S(2)}) collective-permute-start(bf16[16,2,8,128]{3,2,1,0:T(8,128)(2,1)S(1)} %fusion.4), channel_id=1, source_target_pairs={{0,8},{8,0},{16,24},{24,16},{32,40},{40,32},{48,56},{56,48},{64,72... | collective-permute-start | bytes 196616 | tf_op jit(solution)/shard_map/ppermute | solution.py:11
  535.6 6.8 %collective-permute-start.31 = (bf16[16,1,8,128]{3,2,1,0:T(8,128)(2,1)S(1)}, bf16[16,1,8,128]{3,2,1,0:T(8,128)(2,1)S(1)}, u32[]{:S(2)}, u32[]{:S(2)}) collective-permute-start(bf16[16,1,8,128]{3,2,1,0:T(8,128)(2,1)S(1)} %dynamic-slice_convert_fusion.6), channel_id=1, source_target_pairs={{0,16},{8,24},{16,0},{24,8},{32,48},{40,56},{48,32},{56,40},{64,80... | collective-permute-start | bytes 98312 | tf_op jit(solution)/shard_map/ppermute | solution.py:11
  (10 other events, 193.3 us)
Sparse Core Ops, SparseCore 0:
  67.0 73.0 all-reduce.10
  225.6 71.9 all-reduce.12
where the time goes:
time: 552 us; the launch traced here: 550 us
  waiting for transfers between devices  261 us (47%)
  blocking collectives  138 us (25%)
  starting transfers between devices  104 us (19%)
  local copies, waits for them, and re-layouts  17.1 us (3%)
  between operations  14.9 us (3%)
  other arithmetic  7.5 us (1%)
  matrix products  7.2 us (1%)
    unnamed x4, waiting for transfers between devices  145 us
    ppermute x32, waiting for transfers between devices, partner(): lax.ppermute(value, axis, [(i, i ^ 1 << stride) for i in range(lax.axis_s...  116 us
    ppermute x32, starting transfers between devices, partner(): lax.ppermute(value, axis, [(i, i ^ 1 << stride) for i in range(lax.axis_s...  104 us
    unnamed x3, blocking collectives  80.7 us
    all_gather x5, blocking collectives, column_join(): gathered = lax.all_gather(pieces, 'col', axis=1, tiled=True)  57 us
  transfers between devices with their start and end apart: 34, of which 33 were waited for; matrix products, arithmetic and copies ran while one was open for 2% of the time, Pallas kernels for 0%

commit v1 on v0

--- a/solution.py
+++ b/solution.py
@@ -44,7 +44,8 @@
 
 
 def column_join(pieces):
-    gathered = lax.all_gather(pieces, "col", axis=1, tiled=True)
+    sent = jnp.stack([pieces] * lax.axis_size("col"))
+    gathered = jnp.concatenate(lax.all_to_all(sent, "col", 0, 0), axis=1)
     return gathered.reshape(-1, gathered.shape[-1])
 
 

time: 552 us -> 541 us (0.980)
  blocking collectives: 138 us -> 118 us
  waiting for transfers between devices: 261 us -> 267 us
    all_gather x5 -> x0, blocking collectives: 57 us -> none  [column_join(): gathered = lax.all_gather(pieces, 'col', axis=1, tiled=True)]
    all_to_all x0 -> x4, blocking collectives: none -> 36.8 us  [column_join(): gathered = jnp.concatenate(lax.all_to_all(sent, 'col', 0, 0), axis=1)]
    all_to_all x0 -> x1, waiting for transfers between devices: none -> 5.54 us  [column_join(): gathered = jnp.concatenate(lax.all_to_all(sent, 'col', 0, 0), axis=1)]
  transfers between devices with their start and end apart: 34 -> 35, of which waited for: 33 -> 34; matrix products, arithmetic and copies ran while one was open for 2% -> 2% of each run, Pallas kernels for 0% -> 0%
where the time goes in v1:
time: 541 us; the launch traced here: 539 us
  waiting for transfers between devices  267 us (49%)
  blocking collectives  118 us (22%)
  starting transfers between devices  107 us (20%)
  local copies, waits for them, and re-layouts  17.6 us (3%)
  between operations  14.9 us (3%)
  other arithmetic  7.5 us (1%)
  matrix products  7.24 us (1%)
    unnamed x4, waiting for transfers between devices  145 us
    ppermute x32, waiting for transfers between devices, partner(): lax.ppermute(value, axis, [(i, i ^ 1 << stride) for i in range(lax.axis_s...  116 us
    ppermute x32, starting transfers between devices, partner(): lax.ppermute(value, axis, [(i, i ^ 1 << stride) for i in range(lax.axis_s...  104 us
    unnamed x3, blocking collectives  80.8 us
    all_to_all x4, blocking collectives, column_join(): gathered = jnp.concatenate(lax.all_to_all(sent, 'col', 0, 0), axis=1)  36.8 us
  transfers between devices with their start and end apart: 35, of which 34 were waited for; matrix products, arithmetic and copies ran while one was open for 2% of the time, Pallas kernels for 0%

profile of v1, /device:TPU:24, one launch (start us, length us, event | category | flops | bytes accessed | tf_op | source)
XLA Modules:
  0.0 539.1 jit_solution(15964203903044045142)
XLA Ops:
  13.4 6.0 %collective-permute-start.1 = (bf16[16,2,8,128]{3,2,1,0:T(8,128)(2,1)S(1)}, bf16[16,2,8,128]{3,2,1,0:T(8,128)(2,1)S(1)}, u32[]{:S(2)}, u32[]{:S(2)}) collective-permute-start(bf16[16,2,8,128]{3,2,1,0:T(8,128)(2,1)S(1)} %maximum_select_fusion.5), channel_id=1, source_target_pairs={{0,16},{8,24},{16,0},{24,8},{32,48},{40,56},{48,32},{56,40},{64,80... | collective-permute-start | bytes 196616 | tf_op jit(solution)/shard_map/ppermute | solution.py:11
  22.4 29.2 %all-reduce.14 = bf16[16,8,8,128]{3,2,1,0:T(8,128)(2,1)S(1)} all-reduce(f32[16,8,8,128]{3,2,1,0:T(8,128)S(1)} %bitcast.191), channel_id=2, replica_groups=mesh['row'=64,'col'=8] {'col'}, use_global_device_ids=true, to_apply=%region_0.1.clone | all-reduce | flops 131072 | bytes 786432
  52.2 4.1 collective-permute-start.2
  58.5 4.8 collective-permute-start.3
  67.0 73.1 %all-reduce.11.cloned.1.call-done = f32[16,8,8,128]{3,2,1,0:T(8,128)} async-done(((f32[16,8,8,128]{3,2,1,0:T(8,128)}), f32[16,8,8,128]{3,2,1,0:T(8,128)}) %all-reduce.11.cloned.1.call-update) | async-done | bytes 524304
  141.6 4.7 collective-permute-start.4
  146.3 4.9 collective-permute-done.4
  159.3 4.3 collective-permute-done.6
  163.5 4.8 collective-permute-start.7
  169.0 4.6 collective-permute-done.7
  174.1 26.4 %all-reduce.15 = bf16[8,8,8,128]{3,2,1,0:T(8,128)(2,1)S(1)} all-reduce(f32[8,8,8,128]{3,2,1,0:T(8,128)S(1)} %bitcast.192), channel_id=4, replica_groups=mesh['row'=64,'col'=8] {'col'}, use_global_device_ids=true, to_apply=%region_3.4.clone | all-reduce | flops 65536 | bytes 393216
  213.5 5.2 collective-permute-start.10
  225.7 72.2 %all-reduce.13.cloned.1.call-done = f32[8,8,8,128]{3,2,1,0:T(8,128)} async-done(((f32[8,8,8,128]{3,2,1,0:T(8,128)}), f32[8,8,8,128]{3,2,1,0:T(8,128)}) %all-reduce.13.cloned.1.call-update) | async-done | bytes 262160
  312.9 4.3 collective-permute-done.13
  317.2 4.5 collective-permute-start.14
  321.7 5.2 collective-permute-done.14
  335.0 25.3 %all-reduce.16 = bf16[4,8,8,128]{3,2,1,0:T(8,128)(2,1)} all-reduce(f32[4,8,8,128]{3,2,1,0:T(8,128)S(1)} %bitcast.206), channel_id=6, replica_groups=mesh['row'=64,'col'=8] {'col'}, use_global_device_ids=true, to_apply=%region_6.7.clone | all-reduce | flops 32768 | bytes 196608
  365.6 5.5 %all-to-all-done = bf16[8,4,1,8,128]{4,3,1,2,0:T(8,128)(2,1)S(1)} async-done(((bf16[8,4,1,8,128]{4,3,1,2,0:T(8,128)(2,1)}), bf16[8,4,1,8,128]{4,3,1,2,0:T(8,128)(2,1)S(1)}, u32[]{:S(2)}, u32[]{:S(2)}) %all-to-all-start) | async-done | bytes 65568 | tf_op jit(solution)/shard_map/all_to_all | solution.py:48
  382.6 4.8 collective-permute-done.17
  387.4 4.2 collective-permute-start.18
  391.6 5.4 collective-permute-done.18
  408.7 8.5 %all_to_all.25 = bf16[8,8,1,8,128]{4,3,1,2,0:T(8,128)(2,1)S(1)} all-to-all(bf16[8,8,1,8,128]{4,3,1,2,0:T(8,128)(2,1)S(1)} %stack.11), channel_id=1, replica_groups=mesh['row'=64,'col'=8] {'col'}, dimensions={0} | all-to-all | bytes 262144 | tf_op jit(solution)/shard_map/all_to_all | solution.py:48
  425.7 5.1 collective-permute-done.22
  434.7 5.7 %collective-permute-done.23 = bf16[8,1,8,128]{3,2,1,0:T(8,128)(2,1)S(1)} collective-permute-done((bf16[8,1,8,128]{3,2,1,0:T(8,128)(2,1)S(1)}, bf16[8,1,8,128]{3,2,1,0:T(8,128)(2,1)S(1)}, u32[]{:S(2)}, u32[]{:S(2)}) %collective-permute-start.23) | collective-permute-done | bytes 16416 | tf_op jit(solution)/shard_map/ppermute | solution.py:11
  441.7 8.5 %all_to_all.26 = bf16[8,8,1,8,128]{4,3,1,2,0:T(8,128)(2,1)S(1)} all-to-all(bf16[8,8,1,8,128]{4,3,1,2,0:T(8,128)(2,1)S(1)} %stack.12), channel_id=1, replica_groups=mesh['row'=64,'col'=8] {'col'}, dimensions={0} | all-to-all | bytes 262144 | tf_op jit(solution)/shard_map/all_to_all | solution.py:48
  458.8 4.8 collective-permute-done.25
  467.5 5.7 %collective-permute-done.26 = bf16[8,1,8,128]{3,2,1,0:T(8,128)(2,1)S(1)} collective-permute-done((bf16[8,1,8,128]{3,2,1,0:T(8,128)(2,1)S(1)}, bf16[8,1,8,128]{3,2,1,0:T(8,128)(2,1)S(1)}, u32[]{:S(2)}, u32[]{:S(2)}) %collective-permute-start.26) | collective-permute-done | bytes 16416 | tf_op jit(solution)/shard_map/ppermute | solution.py:11
  477.6 5.7 %collective-permute-done.27 = bf16[8,1,8,128]{3,2,1,0:T(8,128)(2,1)S(1)} collective-permute-done((bf16[8,1,8,128]{3,2,1,0:T(8,128)(2,1)S(1)}, bf16[8,1,8,128]{3,2,1,0:T(8,128)(2,1)S(1)}, u32[]{:S(2)}, u32[]{:S(2)}) %collective-permute-start.27) | collective-permute-done | bytes 16416 | tf_op jit(solution)/shard_map/ppermute | solution.py:11
  483.4 9.9 %all_to_all.27 = bf16[8,16,1,8,128]{4,3,1,2,0:T(8,128)(2,1)S(1)} all-to-all(bf16[8,16,1,8,128]{4,3,1,2,0:T(8,128)(2,1)S(1)} %stack.13), channel_id=1, replica_groups=mesh['row'=64,'col'=8] {'col'}, dimensions={0} | all-to-all | bytes 524288 | tf_op jit(solution)/shard_map/all_to_all | solution.py:48
  502.0 4.8 collective-permute-done.29
  508.2 9.9 %all_to_all.28 = bf16[8,16,1,8,128]{4,3,1,2,0:T(8,128)(2,1)S(1)} all-to-all(bf16[8,16,1,8,128]{4,3,1,2,0:T(8,128)(2,1)S(1)} %stack.14), channel_id=1, replica_groups=mesh['row'=64,'col'=8] {'col'}, dimensions={0} | all-to-all | bytes 524288 | tf_op jit(solution)/shard_map/all_to_all | solution.py:48
  526.8 4.8 collective-permute-done.31
  (165 shorter events, 147.6 us)
Async XLA Ops:
  7.2 132.9 %all-reduce.11.cloned.1.call-start = ((), (), s32[]{:S(2)}) async-start(), calls=%async_computation.5 | async-start | bytes 1048576
  7.2 6.2 %collective-permute-start = (bf16[16,1,8,128]{3,2,1,0:T(8,128)(2,1)}, bf16[16,1,8,128]{3,2,1,0:T(8,128)(2,1)S(1)}, u32[]{:S(2)}, u32[]{:S(2)}) collective-permute-start(bf16[16,1,8,128]{3,2,1,0:T(8,128)(2,1)} %bitcast.226), channel_id=1, source_target_pairs={{0,8},{8,0},{16,24},{24,16},{32,40},{40,32},{48,56},{56,48},{64,72... | collective-permute-start | bytes 98312 | tf_op jit(solution)/shard_map/ppermute | solution.py:11
  13.4 8.3 %collective-permute-start.1 = (bf16[16,2,8,128]{3,2,1,0:T(8,128)(2,1)S(1)}, bf16[16,2,8,128]{3,2,1,0:T(8,128)(2,1)S(1)}, u32[]{:S(2)}, u32[]{:S(2)}) collective-permute-start(bf16[16,2,8,128]{3,2,1,0:T(8,128)(2,1)S(1)} %maximum_select_fusion.5), channel_id=1, source_target_pairs={{0,16},{8,24},{16,0},{24,8},{32,48},{40,56},{48,32},{56,40},{64,80... | collective-permute-start | bytes 196616 | tf_op jit(solution)/shard_map/ppermute | solution.py:11
  52.2 6.3 %collective-permute-start.2 = (bf16[16,1,8,128]{3,2,1,0:T(8,128)(2,1)S(1)}, bf16[16,1,8,128]{3,2,1,0:T(8,128)(2,1)S(1)}, u32[]{:S(2)}, u32[]{:S(2)}) collective-permute-start(bf16[16,1,8,128]{3,2,1,0:T(8,128)(2,1)S(1)} %dynamic-slice_convert_fusion.5), channel_id=1, source_target_pairs={{0,8},{8,0},{16,24},{24,16},{32,40},{40,32},{48,56},{56,48},{64,72... | collective-permute-start | bytes 98312 | tf_op jit(solution)/shard_map/ppermute | solution.py:11
  58.5 7.1 %collective-permute-start.3 = (bf16[16,2,8,128]{3,2,1,0:T(8,128)(2,1)S(1)}, bf16[16,2,8,128]{3,2,1,0:T(8,128)(2,1)S(1)}, u32[]{:S(2)}, u32[]{:S(2)}) collective-permute-start(bf16[16,2,8,128]{3,2,1,0:T(8,128)(2,1)S(1)} %maximum_select_fusion.6), channel_id=1, source_target_pairs={{0,16},{8,24},{16,0},{24,8},{32,48},{40,56},{48,32},{56,40},{64,80... | collective-permute-start | bytes 196616 | tf_op jit(solution)/shard_map/ppermute | solution.py:11
  66.9 230.9 %all-reduce.13.cloned.1.call-start = ((), (), s32[]{:S(2)}) async-start(), calls=%async_computation.6 | async-start | bytes 524288
  141.6 9.5 %collective-permute-start.4 = (bf16[8,1,8,128]{3,2,1,0:T(8,128)(2,1)S(1)}, bf16[8,1,8,128]{3,2,1,0:T(8,128)(2,1)S(1)}, u32[]{:S(2)}, u32[]{:S(2)}) collective-permute-start(bf16[8,1,8,128]{3,2,1,0:T(8,128)(2,1)S(1)} %dynamic-slice_convert_fusion.12), channel_id=1, source_target_pairs={{0,32},{8,40},{16,48},{24,56},{32,0},{40,8},{48,16},{56,24},{64,96... | collective-permute-start | bytes 49160 | tf_op jit(solution)/shard_map/ppermute | solution.py:11
  151.2 5.6 %collective-permute-start.5 = (bf16[8,1,8,128]{3,2,1,0:T(8,128)(2,1)S(1)}, bf16[8,1,8,128]{3,2,1,0:T(8,128)(2,1)S(1)}, u32[]{:S(2)}, u32[]{:S(2)}) collective-permute-start(bf16[8,1,8,128]{3,2,1,0:T(8,128)(2,1)S(1)} %fusion.9), channel_id=1, source_target_pairs={{0,8},{8,0},{16,24},{24,16},{32,40},{40,32},{48,56},{56,48},{64,72... | collective-permute-start | bytes 49160 | tf_op jit(solution)/shard_map/ppermute | solution.py:11
  156.8 6.7 %collective-permute-start.6 = (bf16[8,2,8,128]{3,2,1,0:T(8,128)(2,1)S(1)}, bf16[8,2,8,128]{3,2,1,0:T(8,128)(2,1)S(1)}, u32[]{:S(2)}, u32[]{:S(2)}) collective-permute-start(bf16[8,2,8,128]{3,2,1,0:T(8,128)(2,1)S(1)} %maximum_select_fusion.10), channel_id=1, source_target_pairs={{0,16},{8,24},{16,0},{24,8},{32,48},{40,56},{48,32},{56,40},{64,80... | collective-permute-start | bytes 98312 | tf_op jit(solution)/shard_map/ppermute | solution.py:11
  163.5 10.1 %collective-permute-start.7 = (bf16[8,4,8,128]{3,2,1,0:T(8,128)(2,1)S(1)}, bf16[8,4,8,128]{3,2,1,0:T(8,128)(2,1)S(1)}, u32[]{:S(2)}, u32[]{:S(2)}) collective-permute-start(bf16[8,4,8,128]{3,2,1,0:T(8,128)(2,1)S(1)} %maximum_select_fusion.7), channel_id=1, source_target_pairs={{0,32},{8,40},{16,48},{24,56},{32,0},{40,8},{48,16},{56,24},{64,96... | collective-permute-start | bytes 196616 | tf_op jit(solution)/shard_map/ppermute | solution.py:11
  201.2 5.6 %collective-permute-start.8 = (bf16[8,1,8,128]{3,2,1,0:T(8,128)(2,1)S(1)}, bf16[8,1,8,128]{3,2,1,0:T(8,128)(2,1)S(1)}, u32[]{:S(2)}, u32[]{:S(2)}) collective-permute-start(bf16[8,1,8,128]{3,2,1,0:T(8,128)(2,1)S(1)} %dynamic-slice_convert_fusion.8), channel_id=1, source_target_pairs={{0,8},{8,0},{16,24},{24,16},{32,40},{40,32},{48,56},{56,48},{64,72... | collective-permute-start | bytes 49160 | tf_op jit(solution)/shard_map/ppermute | solution.py:11
  206.8 6.7 %collective-permute-start.9 = (bf16[8,2,8,128]{3,2,1,0:T(8,128)(2,1)S(1)}, bf16[8,2,8,128]{3,2,1,0:T(8,128)(2,1)S(1)}, u32[]{:S(2)}, u32[]{:S(2)}) collective-permute-start(bf16[8,2,8,128]{3,2,1,0:T(8,128)(2,1)S(1)} %maximum_select_fusion.11), channel_id=1, source_target_pairs={{0,16},{8,24},{16,0},{24,8},{32,48},{40,56},{48,32},{56,40},{64,80... | collective-permute-start | bytes 98312 | tf_op jit(solution)/shard_map/ppermute | solution.py:11
  213.5 10.1 %collective-permute-start.10 = (bf16[8,4,8,128]{3,2,1,0:T(8,128)(2,1)S(1)}, bf16[8,4,8,128]{3,2,1,0:T(8,128)(2,1)S(1)}, u32[]{:S(2)}, u32[]{:S(2)}) collective-permute-start(bf16[8,4,8,128]{3,2,1,0:T(8,128)(2,1)S(1)} %maximum_select_fusion.8), channel_id=1, source_target_pairs={{0,32},{8,40},{16,48},{24,56},{32,0},{40,8},{48,16},{56,24},{64,96... | collective-permute-start | bytes 196616 | tf_op jit(solution)/shard_map/ppermute | solution.py:11
  299.3 5.7 %collective-permute-start.11 = (bf16[4,1,8,128]{3,2,1,0:T(8,128)(2,1)S(1)}, bf16[4,1,8,128]{3,2,1,0:T(8,128)(2,1)S(1)}, u32[]{:S(2)}, u32[]{:S(2)}) collective-permute-start(bf16[4,1,8,128]{3,2,1,0:T(8,128)(2,1)S(1)} %dynamic-slice_convert_fusion.14), channel_id=1, source_target_pairs={{0,64},{8,72},{16,80},{24,88},{32,96},{40,104},{48,112},{56,120},{... | collective-permute-start | bytes 24584 | tf_op jit(solution)/shard_map/ppermute | solution.py:11
  310.5 6.7 %collective-permute-start.13 = (bf16[4,2,8,128]{3,2,1,0:T(8,128)(2,1)S(1)}, bf16[4,2,8,128]{3,2,1,0:T(8,128)(2,1)S(1)}, u32[]{:S(2)}, u32[]{:S(2)}) collective-permute-start(bf16[4,2,8,128]{3,2,1,0:T(8,128)(2,1)S(1)} %maximum_select_fusion.14), channel_id=1, source_target_pairs={{0,16},{8,24},{16,0},{24,8},{32,48},{40,56},{48,32},{56,40},{64,80... | collective-permute-start | bytes 49160 | tf_op jit(solution)/shard_map/ppermute | solution.py:11
  317.2 9.7 %collective-permute-start.14 = (bf16[4,4,8,128]{3,2,1,0:T(8,128)(2,1)S(1)}, bf16[4,4,8,128]{3,2,1,0:T(8,128)(2,1)S(1)}, u32[]{:S(2)}, u32[]{:S(2)}) collective-permute-start(bf16[4,4,8,128]{3,2,1,0:T(8,128)(2,1)S(1)} %maximum_select_fusion.12), channel_id=1, source_target_pairs={{0,32},{8,40},{16,48},{24,56},{32,0},{40,8},{48,16},{56,24},{64,96... | collective-permute-start | bytes 98312 | tf_op jit(solution)/shard_map/ppermute | solution.py:11
  326.9 6.2 %collective-permute-start.15 = (bf16[4,8,8,128]{3,2,1,0:T(8,128)(2,1)S(1)}, bf16[4,8,8,128]{3,2,1,0:T(8,128)(2,1)S(1)}, u32[]{:S(2)}, u32[]{:S(2)}) collective-permute-start(bf16[4,8,8,128]{3,2,1,0:T(8,128)(2,1)S(1)} %maximum_select_fusion.9), channel_id=1, source_target_pairs={{0,64},{8,72},{16,80},{24,88},{32,96},{40,104},{48,112},{56,120},{... | collective-permute-start | bytes 196616 | tf_op jit(solution)/shard_map/ppermute | solution.py:11
  362.3 8.9 %all-to-all-start = ((bf16[8,4,1,8,128]{4,3,1,2,0:T(8,128)(2,1)}), bf16[8,4,1,8,128]{4,3,1,2,0:T(8,128)(2,1)S(1)}, u32[]{:S(2)}, u32[]{:S(2)}) async-start(bf16[8,4,1,8,128]{4,3,1,2,0:T(8,128)(2,1)} %stack.10), calls=%async_computation | async-start | bytes 131072 | tf_op jit(solution)/shard_map/all_to_all | solution.py:48
  373.2 6.3 %collective-permute-start.16 = (bf16[4,8,8,128]{3,2,1,0:T(8,128)(2,1)S(1)}, bf16[4,8,8,128]{3,2,1,0:T(8,128)(2,1)}, u32[]{:S(2)}, u32[]{:S(2)}) collective-permute-start(bf16[4,8,8,128]{3,2,1,0:T(8,128)(2,1)S(1)} %fusion), channel_id=1, source_target_pairs={{0,8},{8,0},{16,24},{24,16},{32,40},{40,32},{48,56},{56,48},{64,72... | collective-permute-start | bytes 196616 | tf_op jit(solution)/shard_map/ppermute | solution.py:11
  380.3 7.1 %collective-permute-start.17 = (bf16[4,4,8,128]{3,2,1,0:T(8,128)(2,1)S(1)}, bf16[4,4,8,128]{3,2,1,0:T(8,128)(2,1)S(1)}, u32[]{:S(2)}, u32[]{:S(2)}) collective-permute-start(bf16[4,4,8,128]{3,2,1,0:T(8,128)(2,1)S(1)} %fusion.6), channel_id=1, source_target_pairs={{0,16},{8,24},{16,0},{24,8},{32,48},{40,56},{48,32},{56,40},{64,80... | collective-permute-start | bytes 98312 | tf_op jit(solution)/shard_map/ppermute | solution.py:11
  387.4 9.5 %collective-permute-start.18 = (bf16[4,2,8,128]{3,2,1,0:T(8,128)(2,1)S(1)}, bf16[4,2,8,128]{3,2,1,0:T(8,128)(2,1)S(1)}, u32[]{:S(2)}, u32[]{:S(2)}) collective-permute-start(bf16[4,2,8,128]{3,2,1,0:T(8,128)(2,1)S(1)} %fusion.12), channel_id=1, source_target_pairs={{0,32},{8,40},{16,48},{24,56},{32,0},{40,8},{48,16},{56,24},{64,96... | collective-permute-start | bytes 49160 | tf_op jit(solution)/shard_map/ppermute | solution.py:11
  417.6 6.2 %collective-permute-start.21 = (bf16[8,4,8,128]{3,2,1,0:T(8,128)(2,1)S(1)}, bf16[8,4,8,128]{3,2,1,0:T(8,128)(2,1)S(1)}, u32[]{:S(2)}, u32[]{:S(2)}) collective-permute-start(bf16[8,4,8,128]{3,2,1,0:T(8,128)(2,1)S(1)} %fusion.1), channel_id=1, source_target_pairs={{0,8},{8,0},{16,24},{24,16},{32,40},{40,32},{48,56},{56,48},{64,72... | collective-permute-start | bytes 196616 | tf_op jit(solution)/shard_map/ppermute | solution.py:11
  423.8 7.0 %collective-permute-start.22 = (bf16[8,2,8,128]{3,2,1,0:T(8,128)(2,1)S(1)}, bf16[8,2,8,128]{3,2,1,0:T(8,128)(2,1)S(1)}, u32[]{:S(2)}, u32[]{:S(2)}) collective-permute-start(bf16[8,2,8,128]{3,2,1,0:T(8,128)(2,1)S(1)} %fusion.7), channel_id=1, source_target_pairs={{0,16},{8,24},{16,0},{24,8},{32,48},{40,56},{48,32},{56,40},{64,80... | collective-permute-start | bytes 98312 | tf_op jit(solution)/shard_map/ppermute | solution.py:11
  430.8 9.5 %collective-permute-start.23 = (bf16[8,1,8,128]{3,2,1,0:T(8,128)(2,1)S(1)}, bf16[8,1,8,128]{3,2,1,0:T(8,128)(2,1)S(1)}, u32[]{:S(2)}, u32[]{:S(2)}) collective-permute-start(bf16[8,1,8,128]{3,2,1,0:T(8,128)(2,1)S(1)} %dynamic-slice_convert_fusion.10), channel_id=1, source_target_pairs={{0,32},{8,40},{16,48},{24,56},{32,0},{40,8},{48,16},{56,24},{64,96... | collective-permute-start | bytes 49160 | tf_op jit(solution)/shard_map/ppermute | solution.py:11
  450.7 6.2 %collective-permute-start.24 = (bf16[8,4,8,128]{3,2,1,0:T(8,128)(2,1)S(1)}, bf16[8,4,8,128]{3,2,1,0:T(8,128)(2,1)S(1)}, u32[]{:S(2)}, u32[]{:S(2)}) collective-permute-start(bf16[8,4,8,128]{3,2,1,0:T(8,128)(2,1)S(1)} %fusion.2), channel_id=1, source_target_pairs={{0,8},{8,0},{16,24},{24,16},{32,40},{40,32},{48,56},{56,48},{64,72... | collective-permute-start | bytes 196616 | tf_op jit(solution)/shard_map/ppermute | solution.py:11
  456.9 6.7 %collective-permute-start.25 = (bf16[8,2,8,128]{3,2,1,0:T(8,128)(2,1)S(1)}, bf16[8,2,8,128]{3,2,1,0:T(8,128)(2,1)S(1)}, u32[]{:S(2)}, u32[]{:S(2)}) collective-permute-start(bf16[8,2,8,128]{3,2,1,0:T(8,128)(2,1)S(1)} %fusion.8), channel_id=1, source_target_pairs={{0,16},{8,24},{16,0},{24,8},{32,48},{40,56},{48,32},{56,40},{64,80... | collective-permute-start | bytes 98312 | tf_op jit(solution)/shard_map/ppermute | solution.py:11
  463.6 9.5 %collective-permute-start.26 = (bf16[8,1,8,128]{3,2,1,0:T(8,128)(2,1)S(1)}, bf16[8,1,8,128]{3,2,1,0:T(8,128)(2,1)S(1)}, u32[]{:S(2)}, u32[]{:S(2)}) collective-permute-start(bf16[8,1,8,128]{3,2,1,0:T(8,128)(2,1)S(1)} %dynamic-slice_convert_fusion.9), channel_id=1, source_target_pairs={{0,32},{8,40},{16,48},{24,56},{32,0},{40,8},{48,16},{56,24},{64,96... | collective-permute-start | bytes 49160 | tf_op jit(solution)/shard_map/ppermute | solution.py:11
  473.8 9.5 %collective-permute-start.27 = (bf16[8,1,8,128]{3,2,1,0:T(8,128)(2,1)S(1)}, bf16[8,1,8,128]{3,2,1,0:T(8,128)(2,1)S(1)}, u32[]{:S(2)}, u32[]{:S(2)}) collective-permute-start(bf16[8,1,8,128]{3,2,1,0:T(8,128)(2,1)S(1)} %get-tuple-element.4), channel_id=1, source_target_pairs={{0,32},{8,40},{16,48},{24,56},{32,0},{40,8},{48,16},{56,24},{64,96... | collective-permute-start | bytes 49160 | tf_op jit(solution)/shard_map/ppermute | solution.py:11
  493.8 6.2 %collective-permute-start.28 = (bf16[16,2,8,128]{3,2,1,0:T(8,128)(2,1)S(1)}, bf16[16,2,8,128]{3,2,1,0:T(8,128)(2,1)S(1)}, u32[]{:S(2)}, u32[]{:S(2)}) collective-permute-start(bf16[16,2,8,128]{3,2,1,0:T(8,128)(2,1)S(1)} %fusion.3), channel_id=1, source_target_pairs={{0,8},{8,0},{16,24},{24,16},{32,40},{40,32},{48,56},{56,48},{64,72... | collective-permute-start | bytes 196616 | tf_op jit(solution)/shard_map/ppermute | solution.py:11
  500.1 6.7 %collective-permute-start.29 = (bf16[16,1,8,128]{3,2,1,0:T(8,128)(2,1)S(1)}, bf16[16,1,8,128]{3,2,1,0:T(8,128)(2,1)S(1)}, u32[]{:S(2)}, u32[]{:S(2)}) collective-permute-start(bf16[16,1,8,128]{3,2,1,0:T(8,128)(2,1)S(1)} %dynamic-slice_convert_fusion.7), channel_id=1, source_target_pairs={{0,16},{8,24},{16,0},{24,8},{32,48},{40,56},{48,32},{56,40},{64,80... | collective-permute-start | bytes 98312 | tf_op jit(solution)/shard_map/ppermute | solution.py:11
  518.7 6.2 %collective-permute-start.30 = (bf16[16,2,8,128]{3,2,1,0:T(8,128)(2,1)S(1)}, bf16[16,2,8,128]{3,2,1,0:T(8,128)(2,1)S(1)}, u32[]{:S(2)}, u32[]{:S(2)}) collective-permute-start(bf16[16,2,8,128]{3,2,1,0:T(8,128)(2,1)S(1)} %fusion.4), channel_id=1, source_target_pairs={{0,8},{8,0},{16,24},{24,16},{32,40},{40,32},{48,56},{56,48},{64,72... | collective-permute-start | bytes 196616 | tf_op jit(solution)/shard_map/ppermute | solution.py:11
  524.9 6.7 %collective-permute-start.31 = (bf16[16,1,8,128]{3,2,1,0:T(8,128)(2,1)S(1)}, bf16[16,1,8,128]{3,2,1,0:T(8,128)(2,1)S(1)}, u32[]{:S(2)}, u32[]{:S(2)}) collective-permute-start(bf16[16,1,8,128]{3,2,1,0:T(8,128)(2,1)S(1)} %dynamic-slice_convert_fusion.6), channel_id=1, source_target_pairs={{0,16},{8,24},{16,0},{24,8},{32,48},{40,56},{48,32},{56,40},{64,80... | collective-permute-start | bytes 98312 | tf_op jit(solution)/shard_map/ppermute | solution.py:11
  (13 other events, 247.4 us)
Sparse Core Ops, SparseCore 0:
  67.0 73.0 all-reduce.10
  225.8 72.0 all-reduce.12
